TPU v7x, 32 devices: a whole 2x2x4 slice. The times are simulated.
32 devices in a mesh: grp: 2 (over x), seq: 4 (over y, core), tp: 4 (over z).
Axes of the slice: x: 2, y: 2, z: 4, core: 2. Of those that a mesh axis runs over, the one named last changes fastest.
Arguments:
- prompt: bfloat16 [2048, 5376], P(('grp', 'seq'), 'tp'), parts along dimension 0, may hold values from -8 to 8, as said below
- cont_ids: int32 [16, 64], P('grp'), parts along dimension 0, may hold values from 0 to 131071
- embed: bfloat16 [131072, 5376], P('seq', 'tp'), may hold values from -0.078125 to 0.078125
- pre_gain: float32 [5376], replicated, may hold values from 0.5 to 1.5
- w_query: bfloat16 [5376, 4096], P('seq', 'tp'), may hold values from -0.078125 to 0.078125
- w_keyval: bfloat16 [5376, 2, 2048], P('seq', None, 'tp'), may hold values from -0.078125 to 0.078125
- q_gain: float32 [128], replicated, may hold values from 0.25 to 1.75
- k_gain: float32 [128], replicated, may hold values from 0.25 to 1.75
- w_out: bfloat16 [4096, 5376], P('tp', 'seq'), may hold values from -0.09375 to 0.09375
- post_gain: float32 [5376], replicated, may hold values from 0.5 to 1.5
Outputs:
- prompt_out: bfloat16 [2048, 5376], P(('grp', 'seq'), 'tp'), parts along dimension 0
- cont_out: bfloat16 [16, 64, 5376], P(('grp', 'seq'), None, 'tp'), parts along dimension 0
There are 2 independent parts, one for each index of `grp`. A program takes and returns all parts, laid end to end along the dimension named above; an argument that names none is the same for every part. Nothing has to cross between parts.
Inputs may be any that keep to these rules, and one draw needn't show every extreme that they name: `prompt`: values are rough from entry to entry.
All inputs are finite; a program needn't handle non-finite values.
Results may differ from a plain program's by a relative error of at most 0.014.
Values may be sent and summed in bfloat16 or wider, within the bound.
No kernel may reach another device: no remote copies, remote signals or barrier semaphores. Data moves between devices by JAX's collectives and lax.ppermute only.
A program may use at most 256 MiB of HBM per device.

v0:
```python
import math
import jax
import jax.numpy as jnp
from jax import lax
from jax.sharding import PartitionSpec as P

WINDOW = 1024
eps_norm = 1e-06
query_scalar = 168.0
rope_base = 10000.0


def from_behind(value, axis, by):
    count = lax.axis_size(axis)
    pairs = [(i, i + by) for i in range(count) if 0 <= i + by < count]
    return lax.ppermute(value, axis, pairs)


def from_root(value, axis, root):
    mine = lax.axis_index(axis) == root
    return lax.psum(jnp.where(mine, value, jnp.zeros_like(value)), axis)


def rms_scale(values, gain):
    mean_sq = jnp.mean(values * values, axis=-1, keepdims=True)
    return values * lax.rsqrt(mean_sq + eps_norm) * gain


def rotate(values, positions):
    half = values.shape[-1] // 2
    freqs = rope_base ** (
        -(jnp.arange(half, dtype=jnp.int32).astype(jnp.float32) * 2.0) / values.shape[-1]
    )
    angles = positions.astype(jnp.float32)[:, None] * freqs[None, :]
    cosine = jnp.cos(angles)[:, None, :]
    sine = jnp.sin(angles)[:, None, :]
    first = values[..., :half]
    second = values[..., half:]
    return jnp.concatenate(
        [first * cosine - second * sine, second * cosine + first * sine], axis=-1
    )


def attend(queries, keys, values, allowed):
    rows, heads, width = queries.shape
    kv_heads = keys.shape[1]
    grouped = queries.reshape(rows, kv_heads, heads // kv_heads, width)
    scores = jnp.einsum(
        "qkgd,nkd->kgqn", grouped, keys, preferred_element_type=jnp.float32
    ) * query_scalar ** (-0.5)
    scores = jnp.where(allowed[None, None], scores, -1e30)
    top = jnp.max(scores, axis=-1, keepdims=True)
    weights = jnp.exp(scores - top)
    weights = (weights / jnp.sum(weights, axis=-1, keepdims=True)).astype(jnp.bfloat16)
    mixed = jnp.einsum("kgqn,nkd->qkgd", weights, values, preferred_element_type=jnp.float32)
    return mixed.reshape(rows, heads * width).astype(jnp.bfloat16)


def on_device(
    prompt, cont_ids, embed, pre_gain, w_query, w_keyval, q_gain, k_gain, w_out, post_gain
):
    tok_rows, local_cols = prompt.shape
    n_seq = lax.axis_size("seq")
    n_tp = lax.axis_size("tp")
    seq_index = lax.axis_index("seq")
    tp_index = lax.axis_index("tp")
    full_width = local_cols * n_tp
    cont_count, cont_len = cont_ids.shape
    own_conts = cont_count // n_seq
    cont_rows = own_conts * cont_len
    vocab_rows = embed.shape[0]
    flat_ids = cont_ids.reshape(-1)
    vocab_start = seq_index * vocab_rows
    chosen = flat_ids - vocab_start
    inside = (chosen >= 0) & (chosen < vocab_rows)
    picked = jnp.take(embed, jnp.clip(chosen, 0, vocab_rows - 1), axis=0)
    embedded = lax.psum_scatter(
        jnp.where(inside[:, None], picked.astype(jnp.float32), 0.0).astype(jnp.bfloat16),
        "seq",
        scatter_dimension=0,
        tiled=True,
    ).astype(jnp.float32)
    cont_x = (embedded * math.sqrt(full_width)).astype(jnp.bfloat16)
    rows_x = jnp.concatenate([prompt, cont_x], axis=0)
    whole = lax.all_gather(rows_x, "tp", axis=1, tiled=True)
    normed = rms_scale(whole.astype(jnp.float32), pre_gain).astype(jnp.bfloat16)
    all_rows = normed.shape[0]
    q_cols = w_query.shape[1]
    kv_cols = w_keyval.shape[2]
    query_part = jnp.dot(
        normed,
        lax.all_gather(w_query, "seq", axis=0, tiled=True),
        preferred_element_type=jnp.float32,
    )
    kv_part = jnp.einsum(
        "rd,dcf->rcf",
        normed,
        lax.all_gather(w_keyval, "seq", axis=0, tiled=True),
        preferred_element_type=jnp.float32,
    )
    head_dim = q_gain.shape[0]
    q_heads = q_cols // head_dim
    kv_heads = kv_cols // head_dim
    tokens_total = n_seq * tok_rows
    positions = jnp.concatenate(
        [
            seq_index * tok_rows + jnp.arange(tok_rows, dtype=jnp.int32),
            tokens_total + jnp.arange(cont_rows, dtype=jnp.int32) % cont_len,
        ]
    )
    queries = rotate(
        rms_scale(query_part.reshape(all_rows, q_heads, head_dim), q_gain), positions
    ).astype(jnp.bfloat16)
    keys = rotate(
        rms_scale(kv_part[:, 0].reshape(all_rows, kv_heads, head_dim), k_gain), positions
    ).astype(jnp.bfloat16)
    values = kv_part[:, 1].astype(jnp.bfloat16)
    keyval = jnp.stack([keys.reshape(all_rows, kv_cols), values], axis=1)
    prompt_kv = keyval[:tok_rows]
    cont_kv = keyval[tok_rows:]
    reach = WINDOW // tok_rows
    earlier = []
    moving = prompt_kv
    for step in range(reach):
        moving = from_behind(moving, "seq", 1)
        earlier = [moving] + earlier
    band = jnp.concatenate(earlier + [prompt_kv], axis=0)
    q_pos = positions[:tok_rows]
    key_pos = seq_index * tok_rows - reach * tok_rows + jnp.arange(band.shape[0], dtype=jnp.int32)
    allowed = (
        (key_pos[None, :] <= q_pos[:, None])
        & (key_pos[None, :] > q_pos[:, None] - WINDOW)
        & (key_pos[None, :] >= 0)
    )
    prompt_mix = attend(
        queries[:tok_rows],
        band[:, 0].reshape(-1, kv_heads, head_dim),
        band[:, 1].reshape(-1, kv_heads, head_dim),
        allowed,
    )
    final = from_root(band[band.shape[0] - WINDOW :], "seq", n_seq - 1)
    spots = jnp.arange(cont_len, dtype=jnp.int32)
    allowed_cont = jnp.concatenate(
        [
            jnp.arange(WINDOW, dtype=jnp.int32)[None, :] > spots[:, None],
            spots[None, :] <= spots[:, None],
        ],
        axis=1,
    )
    cont_q = queries[tok_rows:].reshape(own_conts, cont_len, q_heads, head_dim)
    cont_keys = cont_kv.reshape(own_conts, cont_len, 2, kv_cols)

    def one_cont(query_block, key_block):
        joined = jnp.concatenate([final, key_block], axis=0)
        return attend(
            query_block,
            joined[:, 0].reshape(-1, kv_heads, head_dim),
            joined[:, 1].reshape(-1, kv_heads, head_dim),
            allowed_cont,
        )

    cont_mix = jax.vmap(one_cont)(cont_q, cont_keys).reshape(cont_rows, q_cols)
    mixed = jnp.concatenate([prompt_mix, cont_mix], axis=0)
    partial_rows = jnp.dot(
        mixed, lax.all_gather(w_out, "seq", axis=1, tiled=True), preferred_element_type=jnp.float32
    )
    attn_proj = lax.psum_scatter(
        partial_rows.astype(jnp.bfloat16), "tp", scatter_dimension=1, tiled=True
    ).astype(jnp.float32)
    row_sq = lax.psum(jnp.sum(attn_proj * attn_proj, axis=1), "tp")
    factor = lax.rsqrt(row_sq / full_width + eps_norm)
    gain_part = lax.dynamic_slice_in_dim(post_gain, tp_index * local_cols, local_cols)
    result = (rows_x.astype(jnp.float32) + attn_proj * factor[:, None] * gain_part).astype(
        jnp.bfloat16
    )
    return (result[:tok_rows], result[tok_rows:].reshape(own_conts, cont_len, local_cols))


def solution(mesh):
    return jax.shard_map(
        on_device,
        mesh=mesh,
        in_specs=(
            P(("grp", "seq"), "tp"),
            P("grp", None),
            P("seq", "tp"),
            P(),
            P("seq", "tp"),
            P("seq", None, "tp"),
            P(),
            P(),
            P("tp", "seq"),
            P(),
        ),
        out_specs=(P(("grp", "seq"), "tp"), P(("grp", "seq"), None, "tp")),
        check_vma=False,
    )
```

profile of v0, /device:TPU:0, one launch (start us, length us, event | category | flops | bytes accessed | tf_op | source)
XLA Modules:
  0.0 655.2 jit_solution(15897168828762125381)
XLA Ops:
  7.2 0.7 subtract_clamp_fusion
  8.8 106.7 %copy.74 = bf16[32768,1344]{1,0:T(8,128)(2,1)} copy(bf16[32768,1344]{0,1:T(8,128)(2,1)} %param.12) | data formatting | bytes 176160768 | tf_op args[2]
  115.5 15.7 %gather_fusion = bf16[512,1344]{1,0:T(8,128)(2,1)S(1)} fusion(bf16[32768,1344]{1,0:T(8,128)(2,1)} %copy.74, s32[1024]{0:T(1024)S(1)} %pad_clamp_fusion), kind=kCustom, calls=%fused_computation | custom fusion | bytes 2754560 | tf_op jit(solution)/shard_map/jit(_take)/gather | solution.py:76
  132.3 1.5 copy.108
  133.9 31.7 %reduce-scatter.7.cloned.1.call-done = bf16[128,1344]{1,0:T(8,128)(2,1)} async-done(((bf16[512,1344]{1,0:T(8,128)(2,1)}), bf16[128,1344]{1,0:T(8,128)(2,1)}) %reduce-scatter.7.cloned.1.call-update) | async-done | bytes 344080
  165.6 1.2 copy.109
  166.9 2.2 pad_maximum_fusion.1
  169.2 1.9 copy.76
  172.2 0.8 multiply_cosine_fusion
  172.9 76.0 %all-gather.5.cloned.1.call-done = bf16[384,5376]{0,1:T(8,128)(2,1)} async-done(((bf16[384,1344]{0,1:T(8,128)(2,1)}), bf16[384,5376]{0,1:T(8,128)(2,1)}) %all-gather.5.cloned.1.call-update) | async-done | bytes 4128784 | tf_op jit(solution)/shard_map/all_gather | solution.py:85
  249.0 3.1 fusion.3
  252.1 70.1 %all-gather.7.cloned.1.call-done = bf16[5376,2,512]{2,0,1:T(8,128)(2,1)} async-done(((bf16[1344,2,512]{2,0,1:T(8,128)(2,1)}), bf16[5376,2,512]{2,0,1:T(8,128)(2,1)}) %all-gather.7.cloned.1.call-update) | async-done | bytes 11010064 | tf_op jit(solution)/shard_map/all_gather | solution.py:98
  322.2 9.9 %fusion.12 = f32[384,2,512]{2,0,1:T(8,128)S(1)} fusion(bf16[5376,2,512]{2,0,1:T(8,128)(2,1)} %all-gather.7.cloned.1.call-done, bf16[384,5376]{0,1:T(8,128)(2,1)} %all-gather.5.cloned.1.call-done, f32[5376]{0:T(1024)S(1)} %copy-done.16, f32[384]{0:T(512)S(1)} %add_rsqrt_fusion.3), kind=kOutput, calls=%fused_computation.25 | convolution fusion | flops 4236115968 | bytes 16734720 | tf_op jit(solution)/shard_map/rd,dcf->rcf/dot_general | solution.py:95
  335.0 2.2 collective-permute-start
  337.2 2.2 collective-permute-done
  339.5 17.3 %collective-permute-start.1 = (bf16[256,2,512]{2,0,1:T(8,128)(2,1)S(1)}, bf16[256,2,512]{2,0,1:T(8,128)(2,1)S(1)}, u32[]{:S(2)}, u32[]{:S(2)}) collective-permute-start(bf16[256,2,512]{2,0,1:T(8,128)(2,1)S(1)} %collective-permute-done), channel_id=1, source_target_pairs={{0,4},{4,8},{8,12},{1,5},{5,9},{9,13},{2,6},{6,10},{10,14},{3,7},{... | collective-permute-start | bytes 1572872 | tf_op jit(solution)/shard_map/ppermute | solution.py:16
  356.8 1.5 collective-permute-done.1
  358.3 20.4 %collective-permute-start.2 = (bf16[256,2,512]{2,0,1:T(8,128)(2,1)S(1)}, bf16[256,2,512]{2,0,1:T(8,128)(2,1)S(1)}, u32[]{:S(2)}, u32[]{:S(2)}) collective-permute-start(bf16[256,2,512]{2,0,1:T(8,128)(2,1)S(1)} %collective-permute-done.1), channel_id=1, source_target_pairs={{0,4},{4,8},{8,12},{1,5},{5,9},{9,13},{2,6},{6,10},{10,14},{3,7},{... | collective-permute-start | bytes 1572872 | tf_op jit(solution)/shard_map/ppermute | solution.py:16
  378.6 1.5 collective-permute-done.2
  380.1 1.8 maximum_select_fusion
  383.8 1.6 and_and_fusion
  385.4 24.4 %all-gather.9.cloned.1.call-done = bf16[5376,1024]{1,0:T(8,128)(2,1)} async-done(((bf16[1344,1024]{1,0:T(8,128)(2,1)}), bf16[5376,1024]{1,0:T(8,128)(2,1)}) %all-gather.9.cloned.1.call-update) | async-done | bytes 11010064 | tf_op jit(solution)/shard_map/all_gather | solution.py:92
  409.7 9.9 %fusion.27 = f32[384,1024]{1,0:T(8,128)S(1)} fusion(bf16[5376,1024]{1,0:T(8,128)(2,1)} %all-gather.9.cloned.1.call-done, bf16[384,5376]{0,1:T(8,128)(2,1)} %all-gather.5.cloned.1.call-done, f32[5376]{0:T(1024)S(1)} %copy-done.16, f32[384]{0:T(512)S(1)} %add_rsqrt_fusion.3), kind=kOutput, calls=%fused_computation.50 | convolution fusion | flops 4236115968 | bytes 16734720 | tf_op jit(solution)/shard_map/dot_general | solution.py:90
  420.0 1.2 multiply_reduce_fusion
  421.2 1.0 copy.80
  422.2 0.8 pad_maximum_fusion.4
  422.9 2.0 copy.86
  425.9 2.1 collective-permute-start.3
  428.6 0.9 pad_maximum_fusion.3
  429.5 1.1 fusion.38
  431.0 1.3 reshape_squeeze.11
  432.3 1.4 copy.100
  433.8 4.8 fusion.65
  438.6 6.8 %fusion.25 = bf16[4,128,2,256]{3,1,2,0:T(8,128)(2,1)} fusion(bf16[1280,4,128,1]{0,2,3,1:T(8,128)(2,1)S(1)} %bitcast.77, f32[4,2,256]{2,1,0:T(2,128)S(1)} %fusion.65, pred[256,1280]{0,1:T(8,128)(4,1)} %and_and_fusion, bf16[256,4,2,128]{3,0,2,1:T(8,128)(2,1)S(1)} %bitcast.80, bf16[1280,4,128,1]{2,1,0,3:T(4,128)(2,1)S(1)} %bitcast.76), kind=kOutput, calls=%fused_computation.48 | convolution fusion | flops 1355549952 | bytes 4005888 | tf_op jit(solution)/shard_map/kgqn,nkd->qkgd/dot_general | solution.py:55
  445.4 24.7 %all-reduce.2.cloned.1.call-done = bf16[1024,2,512]{2,0,1:T(8,128)(2,1)} async-done(((bf16[1024,2,512]{2,0,1:T(8,128)(2,1)}), bf16[1024,2,512]{2,0,1:T(8,128)(2,1)}) %all-reduce.2.cloned.1.call-update) | async-done | bytes 2097168 | tf_op jit(solution)/shard_map/psum | solution.py:21
  470.0 3.0 copy.85
  474.1 1.8 pad_maximum_fusion
  475.9 6.0 exponential_reduce_fusion
  482.0 4.4 fusion.30
  487.0 57.7 %all-gather.11.cloned.1.call-done = bf16[1024,5376]{0,1:T(8,128)(2,1)} async-done(((bf16[1024,1344]{0,1:T(8,128)(2,1)}), bf16[1024,5376]{0,1:T(8,128)(2,1)}) %all-gather.11.cloned.1.call-update) | async-done | bytes 11010064 | tf_op jit(solution)/shard_map/all_gather | solution.py:165
  544.7 11.5 %convolution_convert_fusion = bf16[384,5376]{0,1:T(8,128)(2,1)} fusion(bf16[1024,5376]{0,1:T(8,128)(2,1)} %all-gather.11.cloned.1.call-done, bf16[128,1024]{0,1:T(8,128)(2,1)S(1)} %reshape.287, bf16[256,1024]{0,1:T(8,128)(2,1)S(1)} %bitcast.84), kind=kOutput, calls=%fused_computation.9 | convolution fusion | flops 4231495680 | bytes 15925248 | tf_op jit(solution)/shard_map/dot_general | solution.py:164
  556.3 0.8 dynamic_slice.3
  557.1 75.0 %reduce-scatter.5.cloned.1.call-done = bf16[384,1344]{0,1:T(8,128)(2,1)} async-done(((bf16[384,5376]{0,1:T(8,128)(2,1)}), bf16[384,1344]{0,1:T(8,128)(2,1)}) %reduce-scatter.5.cloned.1.call-update) | async-done | bytes 1032208 | tf_op jit(solution)/shard_map/reduce_scatter | solution.py:167
  632.2 1.5 fusion.18
  633.7 11.0 %psum.15 = f32[384]{0:T(512)S(1)} all-reduce(f32[384]{0:T(512)S(1)} %fusion.18), channel_id=1, replica_groups=mesh['grp'=2,'seq'=4,'tp'=4] {'tp'}, use_global_device_ids=true, to_apply=%region_11.12 | all-reduce | flops 384 | bytes 3072 | tf_op jit(solution)/shard_map/psum | solution.py:170
  644.6 1.6 fusion.21
  646.3 0.9 slice.83
  647.2 0.9 copy.92
  (97 shorter events, 11.9 us)
Async XLA Ops:
  7.2 158.5 %reduce-scatter.7.cloned.1.call-start = ((), (), s32[]{:S(2)}) async-start(), calls=%async_computation.8 | async-start | bytes 1802240
  133.8 35.4 %copy-start = (bf16[1344,2,512]{2,1,0:T(2,128)(2,1)S(1)}, bf16[1344,2,512]{2,1,0:T(2,128)(2,1)}, u32[]{:S(2)}) copy-start(bf16[1344,2,512]{2,1,0:T(2,128)(2,1)} %param.15) | copy-start | bytes 8257540
  133.9 115.1 %all-gather.5.cloned.1.call-start = ((), (), s32[]{:S(2)}) async-start(), calls=%async_computation.2 | async-start | bytes 5160960 | tf_op jit(solution)/shard_map/all_gather | solution.py:85
  169.2 153.1 %all-gather.7.cloned.1.call-start = ((), (), s32[]{:S(2)}) async-start(), calls=%async_computation.3 | async-start | bytes 13762560 | tf_op jit(solution)/shard_map/all_gather | solution.py:98
  171.2 238.6 %all-gather.9.cloned.1.call-start = ((), (), s32[]{:S(2)}) async-start(), calls=%async_computation.4 | async-start | bytes 13762560 | tf_op jit(solution)/shard_map/all_gather | solution.py:92
  171.8 150.4 %copy-start.16 = (f32[5376]{0:T(1024)S(1)}, f32[5376]{0:T(1024)}, u32[]{:S(2)}) copy-start(f32[5376]{0:T(1024)} %param.13) | copy-start | bytes 64516
  171.8 298.3 %all-reduce.2.cloned.1.call-start = ((), (), s32[]{:S(2)}) async-start(), calls=%async_computation.5 | async-start | bytes 4194304 | tf_op jit(solution)/shard_map/psum | solution.py:21
  172.9 160.6 %copy-start.7 = (f32[384,64]{1,0:T(8,128)}, f32[384,64]{1,0:T(8,128)S(1)}, u32[]{:S(2)}) copy-start(f32[384,64]{1,0:T(8,128)S(1)} %get-tuple-element.13) | copy-start | bytes 294916
  332.1 0.9 copy-start.14
  335.0 4.4 collective-permute-start
  339.5 18.8 %collective-permute-start.1 = (bf16[256,2,512]{2,0,1:T(8,128)(2,1)S(1)}, bf16[256,2,512]{2,0,1:T(8,128)(2,1)S(1)}, u32[]{:S(2)}, u32[]{:S(2)}) collective-permute-start(bf16[256,2,512]{2,0,1:T(8,128)(2,1)S(1)} %collective-permute-done), channel_id=1, source_target_pairs={{0,4},{4,8},{8,12},{1,5},{5,9},{9,13},{2,6},{6,10},{10,14},{3,7},{... | collective-permute-start | bytes 1572872 | tf_op jit(solution)/shard_map/ppermute | solution.py:16
  358.3 23.7 %copy-start.2 = (bf16[256,2,512]{2,0,1:T(8,128)(2,1)}, bf16[256,2,512]{2,0,1:T(8,128)(2,1)S(1)}, u32[]{:S(2)}) copy-start(bf16[256,2,512]{2,0,1:T(8,128)(2,1)S(1)} %collective-permute-done.1) | copy-start | bytes 1572868
  358.3 21.8 %collective-permute-start.2 = (bf16[256,2,512]{2,0,1:T(8,128)(2,1)S(1)}, bf16[256,2,512]{2,0,1:T(8,128)(2,1)S(1)}, u32[]{:S(2)}, u32[]{:S(2)}) collective-permute-start(bf16[256,2,512]{2,0,1:T(8,128)(2,1)S(1)} %collective-permute-done.1), channel_id=1, source_target_pairs={{0,4},{4,8},{8,12},{1,5},{5,9},{9,13},{2,6},{6,10},{10,14},{3,7},{... | collective-permute-start | bytes 1572872 | tf_op jit(solution)/shard_map/ppermute | solution.py:16
  380.1 1.8 copy-start.4
  381.9 162.8 %all-gather.11.cloned.1.call-start = ((), (), s32[]{:S(2)}) async-start(), calls=%async_computation.6 | async-start | bytes 13762560 | tf_op jit(solution)/shard_map/all_gather | solution.py:165
  382.5 249.6 %reduce-scatter.5.cloned.1.call-start = ((), (), s32[]{:S(2)}) async-start(), calls=%async_computation.7 | async-start | bytes 5160960 | tf_op jit(solution)/shard_map/reduce_scatter | solution.py:167
  420.0 4.9 copy-start.15
  424.9 1.0 copy-start.5
  424.9 3.1 copy-start.8
  425.9 4.7 collective-permute-start.3
  428.6 2.1 copy-start.3
  431.0 2.8 copy-start.11
  432.3 1.5 copy-start.9
  433.8 4.8 copy-start.10
  473.0 1.0 copy-start.6
  474.1 1.8 copy-start.12
  474.1 1.8 copy-start.13
  482.0 62.8 %copy-start.17 = (bf16[4,128,2,256]{3,1,2,0:T(8,128)(2,1)S(1)}, bf16[4,128,2,256]{3,1,2,0:T(8,128)(2,1)}, u32[]{:S(2)}) copy-start(bf16[4,128,2,256]{3,1,2,0:T(8,128)(2,1)} %fusion.25) | copy-start | bytes 1572868
  556.2 88.4 %copy-start.1 = (bf16[256,1344]{0,1:T(8,128)(2,1)S(1)}, bf16[256,1344]{0,1:T(8,128)(2,1)}, u32[]{:S(2)}) copy-start(bf16[256,1344]{0,1:T(8,128)(2,1)} %param.10) | copy-start | bytes 2064388
Sparse Core Ops, SparseCore 0:
  134.0 31.5 reduce-scatter.6
  169.3 79.6 all-gather.4
  250.5 71.6 all-gather.6
  323.6 86.0 all-gather.8
  412.0 58.0 all-reduce.1
  471.5 73.2 all-gather.10
  556.4 75.7 reduce-scatter.4
where the time goes:
time: 663 us; the launch traced here: 655 us
  waiting for transfers between devices  366 us (55%)
  local copies, waits for them, and re-layouts  143 us (22%)
  matrix products  53.3 us (8%)
  starting transfers between devices  43 us (6%)
  other arithmetic  24.2 us (4%)
  between operations  14.9 us (2%)
  blocking collectives  11 us (2%)
    unnamed x45, local copies, waits for them, and re-layouts  113 us
    all_gather x1, waiting for transfers between devices, on_device(): whole = lax.all_gather(rows_x, 'tp', axis=1, tiled=True)  76 us
    reduce_scatter x1, waiting for transfers between devices, on_device(): lax.psum_scatter(partial_rows.astype(jnp.bfloat16), 'tp', scatter_dimensi...  75 us
    all_gather x1, waiting for transfers between devices, on_device(): lax.all_gather(w_keyval, 'seq', axis=0, tiled=True)  70.1 us
    all_gather x1, waiting for transfers between devices, on_device(): lax.all_gather(w_out, 'seq', axis=1, tiled=True)  57.7 us
    ppermute x4, starting transfers between devices, from_behind(): return lax.ppermute(value, axis, pairs)  41.9 us
    unnamed x8, waiting for transfers between devices  32.8 us
    psum x1, waiting for transfers between devices, from_root(): return lax.psum(jnp.where(mine, value, jnp.zeros_like(value)), axis)  24.7 us
  transfers between devices with their start and end apart: 11, of which 10 were waited for; matrix products, arithmetic and copies ran while one was open for 11% of the time, Pallas kernels for 0%

commit v1 on v0

--- a/solution.py
+++ b/solution.py
@@ -82,7 +82,12 @@
     ).astype(jnp.float32)
     cont_x = (embedded * math.sqrt(full_width)).astype(jnp.bfloat16)
     rows_x = jnp.concatenate([prompt, cont_x], axis=0)
-    whole = lax.all_gather(rows_x, "tp", axis=1, tiled=True)
+    ring = [rows_x]
+    for hop in range(3):
+        ring.append(lax.ppermute(ring[-1], "tp", [(dev, (dev + 1) % 4) for dev in range(4)]))
+    whole = jnp.roll(
+        jnp.concatenate(ring[::-1], axis=1), (lax.axis_index("tp") + 1) * ring[0].shape[1], axis=1
+    )
     normed = rms_scale(whole.astype(jnp.float32), pre_gain).astype(jnp.bfloat16)
     all_rows = normed.shape[0]
     q_cols = w_query.shape[1]

time: 663 us -> 576 us (0.87)
  waiting for transfers between devices: 366 us -> 247 us
  local copies, waits for them, and re-layouts: 143 us -> 159 us
  starting transfers between devices: 43 us -> 56.4 us
    all_gather x1 -> x0, waiting for transfers between devices: 76 us -> none  [on_device(): whole = lax.all_gather(rows_x, 'tp', axis=1, tiled=True)]
    ppermute x0 -> x3, waiting for transfers between devices: none -> 73.7 us  [on_device(): lax.ppermute(ring[-1], 'tp', [(dev, (dev + 1) % 4) for dev in range(4)])]
    all_gather x1, waiting for transfers between devices: 70.1 us -> 0.01 us  [on_device(): lax.all_gather(w_keyval, 'seq', axis=0, tiled=True)]
    all_gather x1, waiting for transfers between devices: 24.4 us -> 0.19 us  [on_device(): lax.all_gather(w_query, 'seq', axis=0, tiled=True)]
    psum x1, waiting for transfers between devices: 24.7 us -> 10.5 us  [from_root(): return lax.psum(jnp.where(mine, value, jnp.zeros_like(value)), axis)]
    ppermute x4, starting transfers between devices: 41.9 us -> 53.8 us  [from_behind(): return lax.ppermute(value, axis, pairs)]
    unnamed x45 -> x53, local copies, waits for them, and re-layouts: 113 us -> 124 us
    unnamed x8 -> x7, waiting for transfers between devices: 32.8 us -> 27.3 us
  transfers between devices with their start and end apart: 11 -> 13, of which waited for: 10 -> 11; matrix products, arithmetic and copies ran while one was open for 11% -> 17% of each run, Pallas kernels for 0% -> 0%
where the time goes in v1:
time: 576 us; the launch traced here: 568 us
  waiting for transfers between devices  247 us (43%)
  local copies, waits for them, and re-layouts  159 us (28%)
  starting transfers between devices  56.4 us (10%)
  matrix products  53.4 us (9%)
  other arithmetic  25.7 us (4%)
  between operations  14.9 us (3%)
  blocking collectives  11 us (2%)
    unnamed x53, local copies, waits for them, and re-layouts  124 us
    reduce_scatter x1, waiting for transfers between devices, on_device(): lax.psum_scatter(partial_rows.astype(jnp.bfloat16), 'tp', scatter_dimensi...  75.1 us
    ppermute x3, waiting for transfers between devices, on_device(): lax.ppermute(ring[-1], 'tp', [(dev, (dev + 1) % 4) for dev in range(4)])  73.7 us
    all_gather x1, waiting for transfers between devices, on_device(): lax.all_gather(w_out, 'seq', axis=1, tiled=True)  56.2 us
    ppermute x4, starting transfers between devices, from_behind(): return lax.ppermute(value, axis, pairs)  53.8 us
    unnamed x7, waiting for transfers between devices  27.3 us
    gather x2, local copies, waits for them, and re-layouts, on_device(): picked = jnp.take(embed, jnp.clip(chosen, 0, vocab_rows - 1), axis=0)  17.1 us
    dot_general x2, matrix products, attend(): jnp.einsum('kgqn,nkd->qkgd', weights, values, preferred_element_type=jnp....  12.1 us
  transfers between devices with their start and end apart: 13, of which 11 were waited for; matrix products, arithmetic and copies ran while one was open for 17% of the time, Pallas kernels for 0%

profile of v1, /device:TPU:0, one launch (start us, length us, event | category | flops | bytes accessed | tf_op | source)
XLA Modules:
  0.0 567.9 jit_solution(14346635820245175479)
XLA Ops:
  8.8 106.8 %copy.74 = bf16[32768,1344]{1,0:T(8,128)(2,1)} copy(bf16[32768,1344]{0,1:T(8,128)(2,1)} %param.12) | data formatting | bytes 176160768 | tf_op args[2]
  115.6 16.5 %gather_fusion = bf16[512,1344]{1,0:T(8,128)(2,1)S(1)} fusion(bf16[32768,1344]{1,0:T(8,128)(2,1)} %copy.74, s32[1024]{0:T(1024)S(1)} %pad_clamp_fusion), kind=kCustom, calls=%fused_computation | custom fusion | bytes 2754560 | tf_op jit(solution)/shard_map/jit(_take)/gather | solution.py:76
  133.2 1.5 copy.108
  134.8 3.7 copy.76
  139.4 26.0 %reduce-scatter.7.cloned.1.call-done = bf16[128,1344]{1,0:T(8,128)(2,1)} async-done(((bf16[512,1344]{1,0:T(8,128)(2,1)}), bf16[128,1344]{1,0:T(8,128)(2,1)}) %reduce-scatter.7.cloned.1.call-update) | async-done | bytes 344080
  165.4 1.2 copy.109
  166.8 1.5 collective-permute-start
  168.3 24.7 %collective-permute-done = bf16[384,1344]{0,1:T(8,128)(2,1)S(1)} collective-permute-done((bf16[384,1344]{0,1:T(8,128)(2,1)S(1)}, bf16[384,1344]{0,1:T(8,128)(2,1)S(1)}, u32[]{:S(2)}, u32[]{:S(2)}) %collective-permute-start) | collective-permute-done | bytes 1032224 | tf_op jit(solution)/shard_map/ppermute | solution.py:87
  193.0 25.3 %collective-permute-done.1 = bf16[384,1344]{0,1:T(8,128)(2,1)S(1)} collective-permute-done((bf16[384,1344]{0,1:T(8,128)(2,1)S(1)}, bf16[384,1344]{0,1:T(8,128)(2,1)S(1)}, u32[]{:S(2)}, u32[]{:S(2)}) %collective-permute-start.1) | collective-permute-done | bytes 1032224 | tf_op jit(solution)/shard_map/ppermute | solution.py:87
  219.4 23.7 %collective-permute-done.2 = bf16[384,1344]{0,1:T(8,128)(2,1)} collective-permute-done((bf16[384,1344]{0,1:T(8,128)(2,1)S(1)}, bf16[384,1344]{0,1:T(8,128)(2,1)}, u32[]{:S(2)}, u32[]{:S(2)}) %collective-permute-start.2) | collective-permute-done | bytes 1032224 | tf_op jit(solution)/shard_map/ppermute | solution.py:87
  243.1 2.3 constant_dynamic-update-slice_fusion.7
  245.4 1.1 constant_dynamic-update-slice_fusion.6
  246.5 1.1 constant_dynamic-update-slice_fusion.5
  247.6 1.1 constant_dynamic-update-slice_fusion.4
  248.8 2.4 constant_dynamic-update-slice_fusion.3
  253.4 1.1 constant_dynamic-update-slice_fusion
  254.5 3.9 fusion.3
  258.5 10.1 %fusion.12 = f32[384,2,512]{2,0,1:T(8,128)S(1)} fusion(bf16[5376,2,512]{2,0,1:T(8,128)(2,1)} %all-gather.4.cloned.1.call-done, f32[5376]{0:T(1024)S(1)} %copy-done.18, f32[384]{0:T(512)S(1)} %add_rsqrt_fusion.3, bf16[384,10752]{0,1:T(8,128)(2,1)} %constant_dynamic-update-slice_fusion, s32[]{:T(128)S(6)} %select_n.69), kind=kOutput, calls=%fused_computation.25 | convolution fusion | flops 4236115968 | bytes 16734724 | tf_op jit(solution)/shard_map/rd,dcf->rcf/dot_general | solution.py:100
  271.5 1.3 collective-permute-start.3
  272.9 1.5 collective-permute-done.3
  274.3 20.0 %collective-permute-start.4 = (bf16[256,2,512]{2,0,1:T(8,128)(2,1)S(1)}, bf16[256,2,512]{2,0,1:T(8,128)(2,1)S(1)}, u32[]{:S(2)}, u32[]{:S(2)}) collective-permute-start(bf16[256,2,512]{2,0,1:T(8,128)(2,1)S(1)} %collective-permute-done.3), channel_id=1, source_target_pairs={{0,4},{4,8},{8,12},{1,5},{5,9},{9,13},{2,6},{6,10},{10,14},{3,7},{... | collective-permute-start | bytes 1572872 | tf_op jit(solution)/shard_map/ppermute | solution.py:16
  294.3 1.5 collective-permute-done.4
  295.8 20.4 %collective-permute-start.5 = (bf16[256,2,512]{2,0,1:T(8,128)(2,1)S(1)}, bf16[256,2,512]{2,0,1:T(8,128)(2,1)S(1)}, u32[]{:S(2)}, u32[]{:S(2)}) collective-permute-start(bf16[256,2,512]{2,0,1:T(8,128)(2,1)S(1)} %collective-permute-done.4), channel_id=1, source_target_pairs={{0,4},{4,8},{8,12},{1,5},{5,9},{9,13},{2,6},{6,10},{10,14},{3,7},{... | collective-permute-start | bytes 1572872 | tf_op jit(solution)/shard_map/ppermute | solution.py:16
  316.2 1.5 collective-permute-done.5
  317.7 2.9 maximum_select_fusion
  321.9 1.6 and_and_fusion
  323.7 10.0 %fusion.35 = f32[384,1024]{1,0:T(8,128)S(1)} fusion(bf16[5376,1024]{1,0:T(8,128)(2,1)} %all-gather.6.cloned.1.call-done, f32[5376]{0:T(1024)S(1)} %copy-done.18, f32[384]{0:T(512)S(1)} %add_rsqrt_fusion.3, bf16[384,10752]{0,1:T(8,128)(2,1)} %constant_dynamic-update-slice_fusion, s32[]{:T(128)S(6)} %select_n.69), kind=kOutput, calls=%fused_computation.64 | convolution fusion | flops 4236115968 | bytes 16734724 | tf_op jit(solution)/shard_map/dot_general | solution.py:95
  334.0 1.2 multiply_reduce_fusion
  336.9 2.0 copy.86
  339.9 12.2 %collective-permute-start.6 = (bf16[256,2,512]{2,0,1:T(8,128)(2,1)S(1)}, bf16[256,2,512]{2,0,1:T(8,128)(2,1)S(1)}, u32[]{:S(2)}, u32[]{:S(2)}) collective-permute-start(bf16[256,2,512]{2,0,1:T(8,128)(2,1)S(1)} %copy-done.6), channel_id=1, source_target_pairs={{0,4},{4,8},{8,12},{1,5},{5,9},{9,13},{2,6},{6,10},{10,14},{3,7},{... | collective-permute-start | bytes 1572872 | tf_op jit(solution)/shard_map/ppermute | solution.py:16
  353.6 1.1 fusion.38
  355.0 1.2 fusion.64
  356.2 3.8 reshape_squeeze.11
  360.1 1.4 copy.100
  361.5 5.1 fusion.67
  366.6 7.1 %fusion.25 = bf16[4,128,2,256]{3,1,2,0:T(8,128)(2,1)} fusion(bf16[1280,4,128,1]{0,2,3,1:T(8,128)(2,1)S(1)} %bitcast.77, f32[4,2,256]{2,1,0:T(2,128)S(1)} %fusion.67, pred[256,1280]{0,1:T(8,128)(4,1)S(1)} %copy-done.15, bf16[256,4,2,128]{3,0,2,1:T(8,128)(2,1)S(1)} %bitcast.80, bf16[1280,4,128,1]{2,1,0,3:T(4,128)(2,1)} %bitcast.76), kind=kOutput, calls=%fused_computation.48 | convolution fusion | flops 1355549952 | bytes 4005888 | tf_op jit(solution)/shard_map/kgqn,nkd->qkgd/dot_general | solution.py:55
  373.7 10.5 %all-reduce.2.cloned.1.call-done = bf16[1024,2,512]{2,0,1:T(8,128)(2,1)} async-done(((bf16[1024,2,512]{2,0,1:T(8,128)(2,1)}), bf16[1024,2,512]{2,0,1:T(8,128)(2,1)}) %all-reduce.2.cloned.1.call-update) | async-done | bytes 2097168 | tf_op jit(solution)/shard_map/psum | solution.py:21
  384.2 3.0 copy.85
  388.3 1.8 pad_maximum_fusion
  390.1 6.0 %exponential_reduce_fusion = (f32[2,4,2,64]{3,2,1,0:T(2,128)S(1)}, f32[2,4,2,64,1088]{4,3,2,1,0:T(8,128)}) fusion(pred[64,1088]{1,0:T(8,128)(4,1)S(1)} %pad_add_fusion, bf16[2,1088,4,128,1]{1,3,4,2,0:T(8,128)(2,1)} %bitcast.74, bf16[2,64,4,2,128]{4,1,0,3,2:T(8,128)(2,1)} %bitcast.82), kind=kOutput, calls=%fused_computation.24 | convolution fusion | flops 289670208 | bytes 7020544 | tf_op jit(solution)/shard_map/vmap()/sub | solution.py:53
  396.1 5.0 fusion.27
  401.1 1.3 copy.107
  402.7 56.2 %all-gather.8.cloned.1.call-done = bf16[1024,5376]{0,1:T(8,128)(2,1)} async-done(((bf16[1024,1344]{0,1:T(8,128)(2,1)}), bf16[1024,5376]{0,1:T(8,128)(2,1)}) %all-gather.8.cloned.1.call-update) | async-done | bytes 11010064 | tf_op jit(solution)/shard_map/all_gather | solution.py:170
  458.9 10.0 %convolution_convert_fusion = bf16[384,5376]{0,1:T(8,128)(2,1)} fusion(bf16[1024,5376]{0,1:T(8,128)(2,1)} %all-gather.8.cloned.1.call-done, bf16[128,1024]{0,1:T(8,128)(2,1)S(1)} %reshape.287, bf16[256,1024]{0,1:T(8,128)(2,1)} %bitcast.84), kind=kOutput, calls=%fused_computation.9 | convolution fusion | flops 4231495680 | bytes 15925248 | tf_op jit(solution)/shard_map/dot_general | solution.py:169
  469.7 75.1 %reduce-scatter.5.cloned.1.call-done = bf16[384,1344]{0,1:T(8,128)(2,1)} async-done(((bf16[384,5376]{0,1:T(8,128)(2,1)}), bf16[384,1344]{0,1:T(8,128)(2,1)}) %reduce-scatter.5.cloned.1.call-update) | async-done | bytes 1032208 | tf_op jit(solution)/shard_map/reduce_scatter | solution.py:172
  544.8 1.5 fusion.18
  546.3 11.0 %psum.15 = f32[384]{0:T(512)S(1)} all-reduce(f32[384]{0:T(512)S(1)} %fusion.18), channel_id=1, replica_groups=mesh['grp'=2,'seq'=4,'tp'=4] {'tp'}, use_global_device_ids=true, to_apply=%region_11.12 | all-reduce | flops 384 | bytes 3072 | tf_op jit(solution)/shard_map/psum | solution.py:175
  557.3 1.6 fusion.21
  (110 shorter events, 19.9 us)
Async XLA Ops:
  7.2 158.2 %reduce-scatter.7.cloned.1.call-start = ((), (), s32[]{:S(2)}) async-start(), calls=%async_computation.7 | async-start | bytes 1802240
  134.8 123.7 %all-gather.4.cloned.1.call-start = ((), (), s32[]{:S(2)}) async-start(), calls=%async_computation.2 | async-start | bytes 13762560 | tf_op jit(solution)/shard_map/all_gather | solution.py:103
  138.6 28.1 %copy-start = (bf16[256,1344]{0,1:T(8,128)(2,1)S(1)}, bf16[256,1344]{0,1:T(8,128)(2,1)}, u32[]{:S(2)}) copy-start(bf16[256,1344]{0,1:T(8,128)(2,1)} %param.10) | copy-start | bytes 2064388
  138.6 185.1 %all-gather.6.cloned.1.call-start = ((), (), s32[]{:S(2)}) async-start(), calls=%async_computation.3 | async-start | bytes 13762560 | tf_op jit(solution)/shard_map/all_gather | solution.py:97
  139.3 244.9 %all-reduce.2.cloned.1.call-start = ((), (), s32[]{:S(2)}) async-start(), calls=%async_computation.4 | async-start | bytes 4194304 | tf_op jit(solution)/shard_map/psum | solution.py:21
  166.8 26.2 %collective-permute-start = (bf16[384,1344]{0,1:T(8,128)(2,1)S(1)}, bf16[384,1344]{0,1:T(8,128)(2,1)S(1)}, u32[]{:S(2)}, u32[]{:S(2)}) collective-permute-start(bf16[384,1344]{0,1:T(8,128)(2,1)S(1)} %pad_maximum_fusion.1), channel_id=1, source_target_pairs={{0,1},{1,2},{2,3},{3,0},{4,5},{5,6},{6,7},{7,4},{8,9},{9,10},{10,1... | collective-permute-start | bytes 3096584 | tf_op jit(solution)/shard_map/ppermute | solution.py:87
  193.0 25.3 %collective-permute-start.1 = (bf16[384,1344]{0,1:T(8,128)(2,1)S(1)}, bf16[384,1344]{0,1:T(8,128)(2,1)S(1)}, u32[]{:S(2)}, u32[]{:S(2)}) collective-permute-start(bf16[384,1344]{0,1:T(8,128)(2,1)S(1)} %collective-permute-done), channel_id=1, source_target_pairs={{0,1},{1,2},{2,3},{3,0},{4,5},{5,6},{6,7},{7,4},{8,9},{9,10},{10,1... | collective-permute-start | bytes 3096584 | tf_op jit(solution)/shard_map/ppermute | solution.py:87
  218.3 24.8 %collective-permute-start.2 = (bf16[384,1344]{0,1:T(8,128)(2,1)S(1)}, bf16[384,1344]{0,1:T(8,128)(2,1)}, u32[]{:S(2)}, u32[]{:S(2)}) collective-permute-start(bf16[384,1344]{0,1:T(8,128)(2,1)S(1)} %collective-permute-done.1), channel_id=1, source_target_pairs={{0,1},{1,2},{2,3},{3,0},{4,5},{5,6},{6,7},{7,4},{8,9},{9,10},{10,1... | collective-permute-start | bytes 3096584 | tf_op jit(solution)/shard_map/ppermute | solution.py:87
  219.4 50.6 %copy-start.9 = (f32[384,64]{1,0:T(8,128)}, f32[384,64]{1,0:T(8,128)S(1)}, u32[]{:S(2)}) copy-start(f32[384,64]{1,0:T(8,128)S(1)} %get-tuple-element.12) | copy-start | bytes 294916
  219.4 50.6 %copy-start.11 = (f32[384,64]{1,0:T(8,128)}, f32[384,64]{1,0:T(8,128)S(1)}, u32[]{:S(2)}) copy-start(f32[384,64]{1,0:T(8,128)S(1)} %get-tuple-element.13) | copy-start | bytes 294916
  253.4 5.1 copy-start.18
  268.6 0.9 copy-start.16
  271.5 1.3 copy-start.8
  271.5 2.8 collective-permute-start.3
  274.3 46.3 %copy-start.1 = (bf16[256,2,512]{2,0,1:T(8,128)(2,1)}, bf16[256,2,512]{2,0,1:T(8,128)(2,1)S(1)}, u32[]{:S(2)}) copy-start(bf16[256,2,512]{2,0,1:T(8,128)(2,1)S(1)} %collective-permute-done.3) | copy-start | bytes 1572868
  274.3 21.5 %collective-permute-start.4 = (bf16[256,2,512]{2,0,1:T(8,128)(2,1)S(1)}, bf16[256,2,512]{2,0,1:T(8,128)(2,1)S(1)}, u32[]{:S(2)}, u32[]{:S(2)}) collective-permute-start(bf16[256,2,512]{2,0,1:T(8,128)(2,1)S(1)} %collective-permute-done.3), channel_id=1, source_target_pairs={{0,4},{4,8},{8,12},{1,5},{5,9},{9,13},{2,6},{6,10},{10,14},{3,7},{... | collective-permute-start | bytes 1572872 | tf_op jit(solution)/shard_map/ppermute | solution.py:16
  295.8 24.8 %copy-start.3 = (bf16[256,2,512]{2,0,1:T(8,128)(2,1)}, bf16[256,2,512]{2,0,1:T(8,128)(2,1)S(1)}, u32[]{:S(2)}) copy-start(bf16[256,2,512]{2,0,1:T(8,128)(2,1)S(1)} %collective-permute-done.4) | copy-start | bytes 1572868
  295.8 21.8 %collective-permute-start.5 = (bf16[256,2,512]{2,0,1:T(8,128)(2,1)S(1)}, bf16[256,2,512]{2,0,1:T(8,128)(2,1)S(1)}, u32[]{:S(2)}, u32[]{:S(2)}) collective-permute-start(bf16[256,2,512]{2,0,1:T(8,128)(2,1)S(1)} %collective-permute-done.4), channel_id=1, source_target_pairs={{0,4},{4,8},{8,12},{1,5},{5,9},{9,13},{2,6},{6,10},{10,14},{3,7},{... | collective-permute-start | bytes 1572872 | tf_op jit(solution)/shard_map/ppermute | solution.py:16
  317.7 3.0 copy-start.5
  320.6 138.3 %all-gather.8.cloned.1.call-start = ((), (), s32[]{:S(2)}) async-start(), calls=%async_computation.5 | async-start | bytes 13762560 | tf_op jit(solution)/shard_map/all_gather | solution.py:170
  321.2 223.6 %reduce-scatter.5.cloned.1.call-start = ((), (), s32[]{:S(2)}) async-start(), calls=%async_computation.6 | async-start | bytes 5160960 | tf_op jit(solution)/shard_map/reduce_scatter | solution.py:172
  334.0 4.9 copy-start.17
  338.9 1.0 copy-start.6
  338.9 13.2 %copy-start.10 = (f32[384,64]{1,0:T(8,128)S(1)}, f32[384,64]{1,0:T(8,128)}, u32[]{:S(2)}) copy-start(f32[384,64]{1,0:T(8,128)} %copy-done.9) | copy-start | bytes 294916
  338.9 13.2 %copy-start.12 = (f32[384,64]{1,0:T(8,128)S(1)}, f32[384,64]{1,0:T(8,128)}, u32[]{:S(2)}) copy-start(f32[384,64]{1,0:T(8,128)} %copy-done.11) | copy-start | bytes 294916
  339.9 14.8 %collective-permute-start.6 = (bf16[256,2,512]{2,0,1:T(8,128)(2,1)S(1)}, bf16[256,2,512]{2,0,1:T(8,128)(2,1)S(1)}, u32[]{:S(2)}, u32[]{:S(2)}) collective-permute-start(bf16[256,2,512]{2,0,1:T(8,128)(2,1)S(1)} %copy-done.6), channel_id=1, source_target_pairs={{0,4},{4,8},{8,12},{1,5},{5,9},{9,13},{2,6},{6,10},{10,14},{3,7},{... | collective-permute-start | bytes 1572872 | tf_op jit(solution)/shard_map/ppermute | solution.py:16
  352.7 2.1 copy-start.4
  353.6 1.3 copy-start.2
  356.2 5.3 copy-start.14
  356.2 5.3 copy-start.15
  361.5 5.1 copy-start.13
  387.2 1.0 copy-start.7
Sparse Core Ops, SparseCore 0:
  134.9 30.4 reduce-scatter.6
  166.9 73.1 all-gather.3
  241.7 81.9 all-gather.5
  325.9 58.2 all-reduce.1
  385.6 73.2 all-gather.7
  469.1 75.6 reduce-scatter.4
